TPU v7x, 128 devices: a whole 4x4x4 slice. The times are simulated.
128 devices in a mesh: space: 8 (over x, core), win: 16 (over z, y).
Axes of the slice: x: 4, y: 4, z: 4, core: 2. Of those that a mesh axis runs over, the one named last changes fastest.
Arguments:
- snapshots: bfloat16 [128, 24576, 256], P('win', 'space'), as said below
- modes: bfloat16 [128, 24576, 256], P('win', 'space'), may hold values from -0.5 to 0.5
- amp_re: float32 [128, 128], P('win'), may hold values from -5 to 5
- amp_im: float32 [128, 128], P('win'), may hold values from -5 to 5
- growth: float32 [128, 128], P('win'), may hold values from -0.01171875 to 0.001953125
- freq: float32 [128, 128], P('win'), may hold values from -3.140625 to 3.140625
- mode_count: int32 [128], P('win'), may hold values from 8 to 128
- slot_window: int32 [128], P('win'), may hold values from 0 to 127, as said below
Outputs:
- gram: float32 [128, 256, 256], P('win')
Inputs may be any that keep to these rules, and one draw needn't show every extreme that they name: slot_window is a permutation of the 128 windows; slot j holds a window of the same position in its block, slot_window[j] % 8 == j % 8; the 8 slots of one block hold windows of 8 different blocks. Each point's snapshots share one scale.
All inputs are finite; a program needn't handle non-finite values.
Results may differ from a plain program's by a relative error of at most 0.0026.
Values may be sent and summed in bfloat16 or wider, within the bound.
A program may use at most 192 MiB of HBM per device.

v0:
```python
import jax
import jax.numpy as jnp
from jax import lax
from jax.sharding import PartitionSpec as P

K = 128
S = 256
WIN_DEV = 8


def coefficients(amp_re, amp_im, growth, freq, mode_count):
    steps = jnp.arange(S).astype(jnp.float32)
    live = (jnp.arange(K, dtype=jnp.int32)[None, :] < mode_count[:, None]).astype(jnp.float32)
    decay = jnp.exp(growth[:, :, None] * steps) * live[:, :, None]
    angle = freq[:, :, None] * steps
    cosine = jnp.cos(angle)
    sine = jnp.sin(angle)
    real_part = (amp_re[:, :, None] * cosine - amp_im[:, :, None] * sine) * decay
    imag_part = (amp_re[:, :, None] * sine + amp_im[:, :, None] * cosine) * decay
    stacked = jnp.stack([real_part, -imag_part], axis=2)
    return stacked.reshape(amp_re.shape[0], 2 * K, S).astype(jnp.bfloat16)


def batch_grams(slabs, vectors, coef):
    recon = jnp.einsum("wpk,wks->wps", vectors, coef, preferred_element_type=jnp.float32)
    resid = (slabs.astype(jnp.float32) - recon).astype(jnp.bfloat16)
    return jnp.einsum("wps,wpt->wst", resid, resid, preferred_element_type=jnp.float32)


def on_device(snapshots, modes, amp_re, amp_im, growth, freq, mode_count, slot_window):
    nblocks = lax.axis_size("win")
    points_all = snapshots.shape[1] * lax.axis_size("space")
    coef = coefficients(amp_re, amp_im, growth, freq, mode_count)
    dest = slot_window // WIN_DEV
    place = slot_window % WIN_DEV
    vec_buf = jnp.zeros((nblocks,) + modes.shape[1:], jnp.bfloat16).at[dest].set(modes)
    coef_buf = jnp.zeros((nblocks, 2 * K, S), jnp.bfloat16).at[dest].set(coef)
    mark_buf = (
        jnp.zeros((nblocks, 128), jnp.bfloat16)
        .at[dest, place]
        .set(jnp.ones((WIN_DEV,), jnp.bfloat16))
    )
    got_vec, got_coef, got_mark = (
        lax.all_to_all(vec_buf, "win", split_axis=0, concat_axis=0, tiled=True),
        lax.all_to_all(coef_buf, "win", split_axis=0, concat_axis=0, tiled=True),
        lax.all_to_all(mark_buf, "win", split_axis=0, concat_axis=0, tiled=True),
    )
    marks = got_mark[:, :WIN_DEV].astype(jnp.int32)
    source = jnp.sum(jnp.arange(nblocks, dtype=jnp.int32)[:, None] * marks, axis=0)
    partial_value = batch_grams(snapshots, got_vec[source], got_coef[source])
    total = lax.psum(partial_value, "space")
    return total / points_all


def solution(mesh):
    return jax.shard_map(
        on_device,
        mesh=mesh,
        in_specs=(
            P("win", "space", None),
            P("win", "space", None),
            P("win", None),
            P("win", None),
            P("win", None),
            P("win", None),
            P("win"),
            P("win"),
        ),
        out_specs=P("win", None, None),
        check_vma=False,
    )
```

profile of v0, /device:TPU:0, one launch (start us, length us, event | category | flops | bytes accessed | tf_op | source)
XLA Modules:
  0.0 555.7 jit_solution(11417734754348130964)
XLA Ops:
  6.5 0.7 fusion.18
  7.2 0.9 scatter_fusion.1
  8.1 0.6 copy.20
  8.7 8.2 %all-to-all-start.1 = ((bf16[16,1,128]{2,1,0:T(2,128)(2,1)}), bf16[16,1,128]{2,1,0:T(2,128)(2,1)S(1)}, u32[]{:S(2)}, u32[]{:S(2)}) async-start(bf16[16,1,128]{2,1,0:T(2,128)(2,1)} %copy.20), calls=%async_computation.1 | async-start | bytes 16384 | tf_op jit(solution)/shard_map/all_to_all | solution.py:46
  16.9 0.7 fusion.14
  17.6 5.3 fusion.9
  22.9 0.1 pad_maximum_fusion
  23.1 0.6 copy.21
  23.6 0.2 copy.22
  23.9 1.5 broadcast_in_dim.14
  25.4 2.8 scatter_fusion.2
  28.2 0.0 all-to-all-done.1
  28.2 7.2 %all-to-all-start.2 = ((bf16[16,256,256]{2,1,0:T(8,128)(2,1)}), bf16[16,256,256]{2,1,0:T(8,128)(2,1)S(1)}, u32[]{:S(2)}, u32[]{:S(2)}) async-start(bf16[16,256,256]{2,1,0:T(8,128)(2,1)} %scatter_fusion.2), calls=%async_computation.2 | async-start | bytes 4194304 | tf_op jit(solution)/shard_map/all_to_all | solution.py:45
  35.5 8.3 %broadcast_in_dim.10 = bf16[16,3072,256]{2,1,0:T(8,128)(2,1)} broadcast(bf16[]{:T(256)} %constant.32.clone.1), dimensions={} | broadcast | bytes 25165826 | tf_op jit(solution)/shard_map/broadcast_in_dim | solution.py:36
  43.8 25.7 %scatter_fusion = bf16[16,3072,256]{2,1,0:T(8,128)(2,1)} fusion(bf16[16,3072,256]{2,1,0:T(8,128)(2,1)} %broadcast_in_dim.10, s32[8]{0:T(128)S(1)} %get-tuple-element.6, bf16[8,3072,256]{2,1,0:T(8,128)(2,1)} %param.9), kind=kCustom, calls=%fused_computation.2 | custom fusion | bytes 37748768 | tf_op jit(solution)/shard_map/scatter | solution.py:36
  69.5 0.0 all-to-all-done.2
  69.5 7.4 %all-to-all-start = ((bf16[16,3072,256]{2,1,0:T(8,128)(2,1)}), bf16[16,3072,256]{2,1,0:T(8,128)(2,1)}, u32[]{:S(2)}, u32[]{:S(2)}) async-start(bf16[16,3072,256]{2,1,0:T(8,128)(2,1)} %scatter_fusion), calls=%async_computation | async-start | bytes 50331648 | tf_op jit(solution)/shard_map/all_to_all | solution.py:44
  76.9 0.0 all-reduce.2.cloned.1.call-start
  77.0 0.6 gather_fusion.1
  77.6 369.2 %all-to-all-done = bf16[16,3072,256]{2,1,0:T(8,128)(2,1)} async-done(((bf16[16,3072,256]{2,1,0:T(8,128)(2,1)}), bf16[16,3072,256]{2,1,0:T(8,128)(2,1)}, u32[]{:S(2)}, u32[]{:S(2)}) %all-to-all-start) | async-done | bytes 25165856 | tf_op jit(solution)/shard_map/all_to_all | solution.py:44
  446.8 14.6 %gather_fusion = bf16[8,3072,256]{2,1,0:T(8,128)(2,1)} fusion(bf16[16,3072,256]{2,1,0:T(8,128)(2,1)} %all-to-all-done, s32[1024]{0:T(1024)S(1)} %pad_clamp_fusion), kind=kCustom, calls=%fused_computation | custom fusion | bytes 25165856 | tf_op jit(solution)/shard_map/gather | solution.py:50
  461.4 19.9 %fusion = f32[8,256,256]{2,1,0:T(8,128)} fusion(bf16[8,3072,256]{2,1,0:T(8,128)(2,1)} %param.8, bf16[8,3072,256]{2,1,0:T(8,128)(2,1)} %gather_fusion, bf16[8,256,256]{2,1,0:T(8,128)(2,1)S(1)} %gather_fusion.1), kind=kOutput, calls=%fused_computation.6 | convolution fusion | flops 6461325312 | bytes 28311552 | tf_op jit(solution)/shard_map/wps,wpt->wst/dot_general | solution.py:27
  481.3 0.0 all-reduce.2.cloned.1.call-update
  481.4 64.4 %all-reduce.2.cloned.1.call-done = f32[8,256,256]{2,1,0:T(8,128)} async-done(((f32[8,256,256]{2,1,0:T(8,128)}), f32[8,256,256]{2,1,0:T(8,128)}) %all-reduce.2.cloned.1.call-update) | async-done | bytes 2097168 | tf_op jit(solution)/shard_map/psum | solution.py:51
  545.8 3.1 broadcast_multiply_fusion
  (7 shorter events, 0.1 us)
Async XLA Ops:
  8.7 19.5 %all-to-all-start.1 = ((bf16[16,1,128]{2,1,0:T(2,128)(2,1)}), bf16[16,1,128]{2,1,0:T(2,128)(2,1)S(1)}, u32[]{:S(2)}, u32[]{:S(2)}) async-start(bf16[16,1,128]{2,1,0:T(2,128)(2,1)} %copy.20), calls=%async_computation.1 | async-start | bytes 16384 | tf_op jit(solution)/shard_map/all_to_all | solution.py:46
  28.2 41.2 %all-to-all-start.2 = ((bf16[16,256,256]{2,1,0:T(8,128)(2,1)}), bf16[16,256,256]{2,1,0:T(8,128)(2,1)S(1)}, u32[]{:S(2)}, u32[]{:S(2)}) async-start(bf16[16,256,256]{2,1,0:T(8,128)(2,1)} %scatter_fusion.2), calls=%async_computation.2 | async-start | bytes 4194304 | tf_op jit(solution)/shard_map/all_to_all | solution.py:45
  69.5 377.3 %all-to-all-start = ((bf16[16,3072,256]{2,1,0:T(8,128)(2,1)}), bf16[16,3072,256]{2,1,0:T(8,128)(2,1)}, u32[]{:S(2)}, u32[]{:S(2)}) async-start(bf16[16,3072,256]{2,1,0:T(8,128)(2,1)} %scatter_fusion), calls=%async_computation | async-start | bytes 50331648 | tf_op jit(solution)/shard_map/all_to_all | solution.py:44
  76.9 468.9 %all-reduce.2.cloned.1.call-start = ((), (), s32[]{:S(2)}) async-start(), calls=%async_computation.3 | async-start | bytes 4194304 | tf_op jit(solution)/shard_map/psum | solution.py:51
Sparse Core Ops, SparseCore 0:
  481.5 64.2 all-reduce.1
where the time goes:
time: 556 us
  waiting for transfers between devices  434 us (78%)
  local copies, waits for them, and re-layouts  55.9 us (10%)
  starting transfers between devices  22.8 us (4%)
  matrix products  19.9 us (4%)
  between operations  13.5 us (2%)
  other arithmetic  9.96 us (2%)
    all_to_all x1, waiting for transfers between devices, on_device(): lax.all_to_all(vec_buf, 'win', split_axis=0, concat_axis=0, tiled=True)  369 us
    psum x1, waiting for transfers between devices, on_device(): total = lax.psum(partial_value, 'space')  64.4 us
    scatter x1, local copies, waits for them, and re-layouts, on_device(): jnp.zeros((nblocks,) + modes.shape[1:], jnp.bfloat16).at[dest].set(modes)  25.7 us
    dot_general x1, matrix products, batch_grams(): jnp.einsum('wps,wpt->wst', resid, resid, preferred_element_type=jnp.float32)  19.9 us
    gather x2, local copies, waits for them, and re-layouts, on_device(): partial_value = batch_grams(snapshots, got_vec[source], got_coef[source])  15.2 us
  transfers between devices with their start and end apart: 4, of which 2 were waited for; matrix products, arithmetic and copies ran while one was open for 8% of the time, Pallas kernels for 0%

commit v1 on v0

--- a/solution.py
+++ b/solution.py
@@ -1,3 +1,4 @@
+import functools
 import jax
 import jax.numpy as jnp
 from jax import lax
@@ -6,6 +7,28 @@
 K = 128
 S = 256
 WIN_DEV = 8
+
+
+def pages_obtain(mine_x, bus_axis):
+    outcome_arr = lax.axis_size(bus_axis)
+    h_now, y = (outcome_arr, lax.axis_index(bus_axis))
+    n_now = mine_x.shape[0] // h_now
+    far_arr = list(mine_x.shape)
+    far_arr[0] = n_now
+    prior = far_arr[0]
+    far_arr[0] = prior * h_now
+    piece_now = jnp.zeros(far_arr, mine_x.dtype)
+    jj = 0
+    while jj < h_now:
+        tmp = lax.dynamic_slice_in_dim(mine_x, (y ^ jj) * n_now, n_now, axis=0)
+        if jj:
+            tmp = lax.ppermute(tmp, bus_axis, [(to_i, to_i ^ jj) for to_i in range(h_now)])
+        piece_now = lax.dynamic_update_slice_in_dim(piece_now, tmp, (y ^ jj) * prior, axis=0)
+        jj += 1
+    return piece_now
+
+
+draft_marks = functools.partial(pages_obtain, bus_axis="win")
 
 
 def coefficients(amp_re, amp_im, growth, freq, mode_count):
@@ -41,7 +64,7 @@
         .set(jnp.ones((WIN_DEV,), jnp.bfloat16))
     )
     got_vec, got_coef, got_mark = (
-        lax.all_to_all(vec_buf, "win", split_axis=0, concat_axis=0, tiled=True),
+        draft_marks(vec_buf),
         lax.all_to_all(coef_buf, "win", split_axis=0, concat_axis=0, tiled=True),
         lax.all_to_all(mark_buf, "win", split_axis=0, concat_axis=0, tiled=True),
     )

time: 556 us -> 659 us (1.19)
  local copies, waits for them, and re-layouts: 55.9 us -> 108 us
  waiting for transfers between devices: 434 us -> 463 us
  starting transfers between devices: 22.8 us -> 45.6 us
    all_to_all x1 -> x0, waiting for transfers between devices: 369 us -> none  [on_device(): lax.all_to_all(vec_buf, 'win', split_axis=0, concat_axis=0, tiled=True)]
    ppermute x0 -> x15, waiting for transfers between devices: none -> 315 us  [pages_obtain(): lax.ppermute(tmp, bus_axis, [(to_i, to_i ^ jj) for to_i in range(h_now)])]
    all_to_all x1, waiting for transfers between devices: 0.01 us -> 82.9 us  [on_device(): lax.all_to_all(mark_buf, 'win', split_axis=0, concat_axis=0, tiled=True)]
    ppermute x0 -> x15, starting transfers between devices: none -> 33 us  [pages_obtain(): lax.ppermute(tmp, bus_axis, [(to_i, to_i ^ jj) for to_i in range(h_now)])]
    dynamic_update_slice x0 -> x15, local copies, waits for them, and re-layouts: none -> 26.2 us  [pages_obtain(): lax.dynamic_update_slice_in_dim(piece_now, tmp, (y ^ jj) * prior, axis=0)]
    dynamic_slice x0 -> x1, local copies, waits for them, and re-layouts: none -> 17.2 us  [pages_obtain(): tmp = lax.dynamic_slice_in_dim(mine_x, (y ^ jj) * n_now, n_now, axis=0)]
    another operation x1 -> x3, local copies, waits for them, and re-layouts: 0.01 us -> 16.9 us
    broadcast_in_dim x1 -> x0, local copies, waits for them, and re-layouts: 8.34 us -> none  [on_device(): jnp.zeros((nblocks,) + modes.shape[1:], jnp.bfloat16).at[dest].set(modes)]
  transfers between devices with their start and end apart: 4 -> 18, of which waited for: 2 -> 6; matrix products, arithmetic and copies ran while one was open for 8% -> 8% of each run, Pallas kernels for 0% -> 0%
where the time goes in v1:
time: 659 us
  waiting for transfers between devices  463 us (70%)
  local copies, waits for them, and re-layouts  108 us (16%)
  starting transfers between devices  45.6 us (7%)
  matrix products  19.9 us (3%)
  between operations  13.7 us (2%)
  other arithmetic  8.51 us (1%)
    ppermute x15, waiting for transfers between devices, pages_obtain(): lax.ppermute(tmp, bus_axis, [(to_i, to_i ^ jj) for to_i in range(h_now)])  315 us
    all_to_all x1, waiting for transfers between devices, on_device(): lax.all_to_all(mark_buf, 'win', split_axis=0, concat_axis=0, tiled=True)  82.9 us
    psum x1, waiting for transfers between devices, on_device(): total = lax.psum(partial_value, 'space')  65 us
    ppermute x15, starting transfers between devices, pages_obtain(): lax.ppermute(tmp, bus_axis, [(to_i, to_i ^ jj) for to_i in range(h_now)])  33 us
    dynamic_update_slice x15, local copies, waits for them, and re-layouts, pages_obtain(): lax.dynamic_update_slice_in_dim(piece_now, tmp, (y ^ jj) * prior, axis=0)  26.2 us
    scatter x1, local copies, waits for them, and re-layouts, on_device(): jnp.zeros((nblocks,) + modes.shape[1:], jnp.bfloat16).at[dest].set(modes)  25.7 us
    dot_general x1, matrix products, batch_grams(): jnp.einsum('wps,wpt->wst', resid, resid, preferred_element_type=jnp.float32)  19.9 us
    dynamic_slice x1, local copies, waits for them, and re-layouts, pages_obtain(): tmp = lax.dynamic_slice_in_dim(mine_x, (y ^ jj) * n_now, n_now, axis=0)  17.2 us
  transfers between devices with their start and end apart: 18, of which 6 were waited for; matrix products, arithmetic and copies ran while one was open for 8% of the time, Pallas kernels for 0%

profile of v1, /device:TPU:0, one launch (start us, length us, event | category | flops | bytes accessed | tf_op | source)
XLA Modules:
  0.0 658.7 jit_solution(2392851222058918429)
XLA Ops:
  7.3 8.4 %broadcast.148.clone = bf16[16,3072,256]{2,1,0:T(8,128)(2,1)} broadcast(bf16[]{:T(256)} %constant.23.clone.1), dimensions={} | broadcast | bytes 25165826 | tf_op jit(solution)/shard_map/broadcast.15
  15.7 25.7 %scatter_fusion = bf16[16,3072,256]{2,1,0:T(8,128)(2,1)} fusion(bf16[16,3072,256]{2,1,0:T(8,128)(2,1)} %broadcast.148.clone, s32[8]{0:T(128)S(1)} %get-tuple-element.6, bf16[8,3072,256]{2,1,0:T(8,128)(2,1)} %param.9), kind=kCustom, calls=%fused_computation.2 | custom fusion | bytes 37748768 | tf_op jit(solution)/shard_map/scatter | solution.py:59
  41.4 8.4 %broadcast.148 = bf16[16,3072,256]{2,1,0:T(8,128)(2,1)} broadcast(bf16[]{:T(256)} %constant.23.clone.1), dimensions={} | broadcast | bytes 25165826 | tf_op jit(solution)/shard_map/broadcast.15
  49.9 17.2 %constant_dynamic-slice_fusion = (bf16[1,3072,256]{2,1,0:T(8,128)(2,1)}, bf16[1,3072,256]{2,1,0:T(8,128)(2,1)}, bf16[1,3072,256]{2,1,0:T(8,128)(2,1)}, bf16[1,30...) fusion(bf16[16,3072,256]{2,1,0:T(8,128)(2,1)} %scatter_fusion, ...), kind=kLoop, calls=%fused_computation.27 | loop fusion | bytes 50331712 | tf_op jit(solution)/shard_map/dynamic_slice | solution.py:23
  67.1 2.0 collective-permute-start
  69.0 2.7 collective-permute-start.1
  71.9 2.3 collective-permute-start.3
  75.7 8.8 %all-to-all-start = ((bf16[16,1,128]{2,1,0:T(2,128)(2,1)}), bf16[16,1,128]{2,1,0:T(2,128)(2,1)S(1)}, u32[]{:S(2)}, u32[]{:S(2)}) async-start(bf16[16,1,128]{2,1,0:T(2,128)(2,1)} %copy.20), calls=%async_computation | async-start | bytes 16384 | tf_op jit(solution)/shard_map/all_to_all | solution.py:69
  84.6 4.5 fusion.9
  90.1 1.5 broadcast_in_dim.11
  91.6 2.8 scatter_fusion.2
  94.4 82.9 %all-to-all-done = bf16[16,1,128]{2,1,0:T(2,128)(2,1)S(1)} async-done(((bf16[16,1,128]{2,1,0:T(2,128)(2,1)}), bf16[16,1,128]{2,1,0:T(2,128)(2,1)S(1)}, u32[]{:S(2)}, u32[]{:S(2)}) %all-to-all-start) | async-done | bytes 4128 | tf_op jit(solution)/shard_map/all_to_all | solution.py:69
  177.3 3.7 all-to-all-start.1
  181.2 4.3 collective-permute-start.5
  185.5 2.8 constant_dynamic-update-slice_fusion.14
  189.6 2.7 constant_dynamic-update-slice_fusion.13
  192.3 2.9 collective-permute-start.7
  195.1 2.7 constant_dynamic-update-slice_fusion.12
  197.8 2.6 constant_dynamic-update-slice_fusion.11
  200.5 6.0 collective-permute-start.9
  206.5 2.7 constant_dynamic-update-slice_fusion.10
  209.2 37.9 %collective-permute-done.5 = bf16[1,3072,256]{2,1,0:T(8,128)(2,1)S(1)} collective-permute-done((bf16[1,3072,256]{2,1,0:T(8,128)(2,1)}, bf16[1,3072,256]{2,1,0:T(8,128)(2,1)S(1)}, u32[]{:S(2)}, u32[]{:S(2)}) %collective-permute-start.5) | collective-permute-done | bytes 1572896 | tf_op jit(solution)/shard_map/ppermute | solution.py:25
  247.1 2.7 collective-permute-start.10
  251.0 50.2 %collective-permute-done.6 = bf16[1,3072,256]{2,1,0:T(8,128)(2,1)S(1)} collective-permute-done((bf16[1,3072,256]{2,1,0:T(8,128)(2,1)}, bf16[1,3072,256]{2,1,0:T(8,128)(2,1)S(1)}, u32[]{:S(2)}, u32[]{:S(2)}) %collective-permute-start.6) | collective-permute-done | bytes 1572896 | tf_op jit(solution)/shard_map/ppermute | solution.py:25
  303.9 104.8 %collective-permute-done.7 = bf16[1,3072,256]{2,1,0:T(8,128)(2,1)S(1)} collective-permute-done((bf16[1,3072,256]{2,1,0:T(8,128)(2,1)}, bf16[1,3072,256]{2,1,0:T(8,128)(2,1)S(1)}, u32[]{:S(2)}, u32[]{:S(2)}) %collective-permute-start.7) | collective-permute-done | bytes 1572896 | tf_op jit(solution)/shard_map/ppermute | solution.py:25
  408.7 2.1 collective-permute-start.12
  412.1 4.2 collective-permute-start.13
  421.2 122.3 %collective-permute-done.11 = bf16[1,3072,256]{2,1,0:T(8,128)(2,1)S(1)} collective-permute-done((bf16[1,3072,256]{2,1,0:T(8,128)(2,1)S(1)}, bf16[1,3072,256]{2,1,0:T(8,128)(2,1)S(1)}, u32[]{:S(2)}, u32[]{:S(2)}) %collective-permute-start.11) | collective-permute-done | bytes 1572896 | tf_op jit(solution)/shard_map/ppermute | solution.py:25
  548.6 14.6 %gather_fusion = bf16[8,3072,256]{2,1,0:T(8,128)(2,1)} fusion(bf16[16,3072,256]{2,1,0:T(8,128)(2,1)} %constant_dynamic-update-slice_fusion, s32[1024]{0:T(1024)S(1)} %pad_clamp_fusion), kind=kCustom, calls=%fused_computation | custom fusion | bytes 25165856 | tf_op jit(solution)/shard_map/gather | solution.py:73
  563.8 19.9 %fusion = f32[8,256,256]{2,1,0:T(8,128)} fusion(bf16[8,3072,256]{2,1,0:T(8,128)(2,1)} %param.8, bf16[8,3072,256]{2,1,0:T(8,128)(2,1)} %gather_fusion, bf16[8,256,256]{2,1,0:T(8,128)(2,1)S(1)} %gather_fusion.1), kind=kOutput, calls=%fused_computation.6 | convolution fusion | flops 6461325312 | bytes 28311552 | tf_op jit(solution)/shard_map/wps,wpt->wst/dot_general | solution.py:50
  583.8 65.0 %all-reduce.2.cloned.1.call-done = f32[8,256,256]{2,1,0:T(8,128)} async-done(((f32[8,256,256]{2,1,0:T(8,128)}), f32[8,256,256]{2,1,0:T(8,128)}) %all-reduce.2.cloned.1.call-update) | async-done | bytes 2097168 | tf_op jit(solution)/shard_map/psum | solution.py:74
  648.7 3.1 broadcast_multiply_fusion
  (67 shorter events, 20.6 us)
Async XLA Ops:
  49.8 34.7 %copy-start.6 = (s32[8]{0:T(128)S(1)}, s32[8]{0:T(128)}, u32[]{:S(2)}) copy-start(s32[8]{0:T(128)} %param.14) | copy-start | bytes 100
  49.8 34.7 %copy-start.7 = (f32[8,128]{1,0:T(8,128)S(1)}, f32[8,128]{1,0:T(8,128)}, u32[]{:S(2)}) copy-start(f32[8,128]{1,0:T(8,128)} %param.12) | copy-start | bytes 12292
  49.8 34.7 %copy-start.8 = (f32[8,128]{1,0:T(8,128)S(1)}, f32[8,128]{1,0:T(8,128)}, u32[]{:S(2)}) copy-start(f32[8,128]{1,0:T(8,128)} %param.11) | copy-start | bytes 12292
  49.8 34.8 %copy-start.9 = (f32[8,128]{1,0:T(8,128)S(1)}, f32[8,128]{1,0:T(8,128)}, u32[]{:S(2)}) copy-start(f32[8,128]{1,0:T(8,128)} %param.13) | copy-start | bytes 12292
  49.9 34.7 %copy-start.10 = (f32[8,128]{1,0:T(8,128)S(1)}, f32[8,128]{1,0:T(8,128)}, u32[]{:S(2)}) copy-start(f32[8,128]{1,0:T(8,128)} %param.10) | copy-start | bytes 12292
  67.1 114.1 %collective-permute-start = (bf16[1,3072,256]{2,1,0:T(8,128)(2,1)}, bf16[1,3072,256]{2,1,0:T(8,128)(2,1)}, u32[]{:S(2)}, u32[]{:S(2)}) collective-permute-start(bf16[1,3072,256]{2,1,0:T(8,128)(2,1)} %get-tuple-element.21), channel_id=1, source_target_pairs={{0,1},{1,0},{2,3},{3,2},{4,5},{5,4},{6,7},{7,6},{8,9},{9,8},{10,11... | collective-permute-start | bytes 4718600 | tf_op jit(solution)/shard_map/ppermute | solution.py:25
  69.0 119.3 %collective-permute-start.1 = (bf16[1,3072,256]{2,1,0:T(8,128)(2,1)}, bf16[1,3072,256]{2,1,0:T(8,128)(2,1)}, u32[]{:S(2)}, u32[]{:S(2)}) collective-permute-start(bf16[1,3072,256]{2,1,0:T(8,128)(2,1)} %get-tuple-element.20), channel_id=1, source_target_pairs={{0,2},{1,3},{2,0},{3,1},{4,6},{5,7},{6,4},{7,5},{8,10},{9,11},{10,... | collective-permute-start | bytes 4718600 | tf_op jit(solution)/shard_map/ppermute | solution.py:25
  71.8 120.5 %collective-permute-start.2 = (bf16[1,3072,256]{2,1,0:T(8,128)(2,1)}, bf16[1,3072,256]{2,1,0:T(8,128)(2,1)}, u32[]{:S(2)}, u32[]{:S(2)}) collective-permute-start(bf16[1,3072,256]{2,1,0:T(8,128)(2,1)} %get-tuple-element.19), channel_id=1, source_target_pairs={{0,3},{1,2},{2,1},{3,0},{4,7},{5,6},{6,5},{7,4},{8,11},{9,10},{10,... | collective-permute-start | bytes 4718600 | tf_op jit(solution)/shard_map/ppermute | solution.py:25
  71.9 126.0 %collective-permute-start.3 = (bf16[1,3072,256]{2,1,0:T(8,128)(2,1)}, bf16[1,3072,256]{2,1,0:T(8,128)(2,1)}, u32[]{:S(2)}, u32[]{:S(2)}) collective-permute-start(bf16[1,3072,256]{2,1,0:T(8,128)(2,1)} %get-tuple-element.18), channel_id=1, source_target_pairs={{0,4},{1,5},{2,6},{3,7},{4,0},{5,1},{6,2},{7,3},{8,12},{9,13},{10,... | collective-permute-start | bytes 4718600 | tf_op jit(solution)/shard_map/ppermute | solution.py:25
  74.2 126.3 %collective-permute-start.4 = (bf16[1,3072,256]{2,1,0:T(8,128)(2,1)}, bf16[1,3072,256]{2,1,0:T(8,128)(2,1)}, u32[]{:S(2)}, u32[]{:S(2)}) collective-permute-start(bf16[1,3072,256]{2,1,0:T(8,128)(2,1)} %get-tuple-element.17), channel_id=1, source_target_pairs={{0,5},{1,4},{2,7},{3,6},{4,1},{5,0},{6,3},{7,2},{8,13},{9,12},{10,... | collective-permute-start | bytes 4718600 | tf_op jit(solution)/shard_map/ppermute | solution.py:25
  75.7 101.7 %all-to-all-start = ((bf16[16,1,128]{2,1,0:T(2,128)(2,1)}), bf16[16,1,128]{2,1,0:T(2,128)(2,1)S(1)}, u32[]{:S(2)}, u32[]{:S(2)}) async-start(bf16[16,1,128]{2,1,0:T(2,128)(2,1)} %copy.20), calls=%async_computation | async-start | bytes 16384 | tf_op jit(solution)/shard_map/all_to_all | solution.py:69
  177.3 385.9 %all-to-all-start.1 = ((bf16[16,256,256]{2,1,0:T(8,128)(2,1)}), bf16[16,256,256]{2,1,0:T(8,128)(2,1)S(1)}, u32[]{:S(2)}, u32[]{:S(2)}) async-start(bf16[16,256,256]{2,1,0:T(8,128)(2,1)} %scatter_fusion.2), calls=%async_computation.1 | async-start | bytes 4194304 | tf_op jit(solution)/shard_map/all_to_all | solution.py:68
  181.1 467.7 %all-reduce.2.cloned.1.call-start = ((), (), s32[]{:S(2)}) async-start(), calls=%async_computation.2 | async-start | bytes 4194304 | tf_op jit(solution)/shard_map/psum | solution.py:74
  181.1 19.4 %copy-start.5 = (bf16[1,3072,256]{2,1,0:T(8,128)(2,1)S(1)}, bf16[1,3072,256]{2,1,0:T(8,128)(2,1)}, u32[]{:S(2)}) copy-start(bf16[1,3072,256]{2,1,0:T(8,128)(2,1)} %get-tuple-element.12) | copy-start | bytes 4718596
  181.1 66.0 %copy-start.4 = (bf16[1,3072,256]{2,1,0:T(8,128)(2,1)S(1)}, bf16[1,3072,256]{2,1,0:T(8,128)(2,1)}, u32[]{:S(2)}) copy-start(bf16[1,3072,256]{2,1,0:T(8,128)(2,1)} %get-tuple-element.11) | copy-start | bytes 4718596
  181.1 120.0 %copy-start.3 = (bf16[1,3072,256]{2,1,0:T(8,128)(2,1)S(1)}, bf16[1,3072,256]{2,1,0:T(8,128)(2,1)}, u32[]{:S(2)}) copy-start(bf16[1,3072,256]{2,1,0:T(8,128)(2,1)} %get-tuple-element.10) | copy-start | bytes 4718596
  181.1 227.6 %copy-start.2 = (bf16[1,3072,256]{2,1,0:T(8,128)(2,1)S(1)}, bf16[1,3072,256]{2,1,0:T(8,128)(2,1)}, u32[]{:S(2)}) copy-start(bf16[1,3072,256]{2,1,0:T(8,128)(2,1)} %get-tuple-element.9) | copy-start | bytes 4718596
  181.2 65.9 %collective-permute-start.5 = (bf16[1,3072,256]{2,1,0:T(8,128)(2,1)}, bf16[1,3072,256]{2,1,0:T(8,128)(2,1)S(1)}, u32[]{:S(2)}, u32[]{:S(2)}) collective-permute-start(bf16[1,3072,256]{2,1,0:T(8,128)(2,1)} %get-tuple-element.16), channel_id=1, source_target_pairs={{0,6},{1,7},{2,4},{3,5},{4,2},{5,3},{6,0},{7,1},{8,14},{9,15},{10,... | collective-permute-start | bytes 4718600 | tf_op jit(solution)/shard_map/ppermute | solution.py:25
  185.5 226.5 %copy-start.1 = (bf16[1,3072,256]{2,1,0:T(8,128)(2,1)S(1)}, bf16[1,3072,256]{2,1,0:T(8,128)(2,1)}, u32[]{:S(2)}) copy-start(bf16[1,3072,256]{2,1,0:T(8,128)(2,1)} %get-tuple-element.8) | copy-start | bytes 4718596
  188.3 229.2 %copy-start = (bf16[1,3072,256]{2,1,0:T(8,128)(2,1)S(1)}, bf16[1,3072,256]{2,1,0:T(8,128)(2,1)}, u32[]{:S(2)}) copy-start(bf16[1,3072,256]{2,1,0:T(8,128)(2,1)} %get-tuple-element.7) | copy-start | bytes 4718596
  188.3 112.8 %collective-permute-start.6 = (bf16[1,3072,256]{2,1,0:T(8,128)(2,1)}, bf16[1,3072,256]{2,1,0:T(8,128)(2,1)S(1)}, u32[]{:S(2)}, u32[]{:S(2)}) collective-permute-start(bf16[1,3072,256]{2,1,0:T(8,128)(2,1)} %get-tuple-element.15), channel_id=1, source_target_pairs={{0,7},{1,6},{2,5},{3,4},{4,3},{5,2},{6,1},{7,0},{8,15},{9,14},{10,... | collective-permute-start | bytes 4718600 | tf_op jit(solution)/shard_map/ppermute | solution.py:25
  192.3 216.4 %collective-permute-start.7 = (bf16[1,3072,256]{2,1,0:T(8,128)(2,1)}, bf16[1,3072,256]{2,1,0:T(8,128)(2,1)S(1)}, u32[]{:S(2)}, u32[]{:S(2)}) collective-permute-start(bf16[1,3072,256]{2,1,0:T(8,128)(2,1)} %get-tuple-element.14), channel_id=1, source_target_pairs={{0,8},{1,9},{2,10},{3,11},{4,12},{5,13},{6,14},{7,15},{8,0},{9,1},... | collective-permute-start | bytes 4718600 | tf_op jit(solution)/shard_map/ppermute | solution.py:25
  197.8 214.2 %collective-permute-start.8 = (bf16[1,3072,256]{2,1,0:T(8,128)(2,1)}, bf16[1,3072,256]{2,1,0:T(8,128)(2,1)S(1)}, u32[]{:S(2)}, u32[]{:S(2)}) collective-permute-start(bf16[1,3072,256]{2,1,0:T(8,128)(2,1)} %get-tuple-element.13), channel_id=1, source_target_pairs={{0,9},{1,8},{2,11},{3,10},{4,13},{5,12},{6,15},{7,14},{8,1},{9,0},... | collective-permute-start | bytes 4718600 | tf_op jit(solution)/shard_map/ppermute | solution.py:25
  200.5 217.0 %collective-permute-start.9 = (bf16[1,3072,256]{2,1,0:T(8,128)(2,1)S(1)}, bf16[1,3072,256]{2,1,0:T(8,128)(2,1)S(1)}, u32[]{:S(2)}, u32[]{:S(2)}) collective-permute-start(bf16[1,3072,256]{2,1,0:T(8,128)(2,1)S(1)} %copy-done.5), channel_id=1, source_target_pairs={{0,10},{1,11},{2,8},{3,9},{4,14},{5,15},{6,12},{7,13},{8,2},{9,3},... | collective-permute-start | bytes 4718600 | tf_op jit(solution)/shard_map/ppermute | solution.py:25
  247.1 172.8 %collective-permute-start.10 = (bf16[1,3072,256]{2,1,0:T(8,128)(2,1)S(1)}, bf16[1,3072,256]{2,1,0:T(8,128)(2,1)S(1)}, u32[]{:S(2)}, u32[]{:S(2)}) collective-permute-start(bf16[1,3072,256]{2,1,0:T(8,128)(2,1)S(1)} %copy-done.4), channel_id=1, source_target_pairs={{0,11},{1,10},{2,9},{3,8},{4,15},{5,14},{6,13},{7,12},{8,3},{9,2},... | collective-permute-start | bytes 4718600 | tf_op jit(solution)/shard_map/ppermute | solution.py:25
  301.1 242.3 %collective-permute-start.11 = (bf16[1,3072,256]{2,1,0:T(8,128)(2,1)S(1)}, bf16[1,3072,256]{2,1,0:T(8,128)(2,1)S(1)}, u32[]{:S(2)}, u32[]{:S(2)}) collective-permute-start(bf16[1,3072,256]{2,1,0:T(8,128)(2,1)S(1)} %copy-done.3), channel_id=1, source_target_pairs={{0,12},{1,13},{2,14},{3,15},{4,8},{5,9},{6,10},{7,11},{8,4},{9,5},... | collective-permute-start | bytes 4718600 | tf_op jit(solution)/shard_map/ppermute | solution.py:25
  408.7 136.0 %collective-permute-start.12 = (bf16[1,3072,256]{2,1,0:T(8,128)(2,1)S(1)}, bf16[1,3072,256]{2,1,0:T(8,128)(2,1)S(1)}, u32[]{:S(2)}, u32[]{:S(2)}) collective-permute-start(bf16[1,3072,256]{2,1,0:T(8,128)(2,1)S(1)} %copy-done.2), channel_id=1, source_target_pairs={{0,13},{1,12},{2,15},{3,14},{4,9},{5,8},{6,11},{7,10},{8,5},{9,4},... | collective-permute-start | bytes 4718600 | tf_op jit(solution)/shard_map/ppermute | solution.py:25
  412.1 133.9 %collective-permute-start.13 = (bf16[1,3072,256]{2,1,0:T(8,128)(2,1)S(1)}, bf16[1,3072,256]{2,1,0:T(8,128)(2,1)S(1)}, u32[]{:S(2)}, u32[]{:S(2)}) collective-permute-start(bf16[1,3072,256]{2,1,0:T(8,128)(2,1)S(1)} %copy-done.1), channel_id=1, source_target_pairs={{0,14},{1,15},{2,12},{3,13},{4,10},{5,11},{6,8},{7,9},{8,6},{9,7},... | collective-permute-start | bytes 4718600 | tf_op jit(solution)/shard_map/ppermute | solution.py:25
  417.5 129.8 %collective-permute-start.14 = (bf16[1,3072,256]{2,1,0:T(8,128)(2,1)S(1)}, bf16[1,3072,256]{2,1,0:T(8,128)(2,1)S(1)}, u32[]{:S(2)}, u32[]{:S(2)}) collective-permute-start(bf16[1,3072,256]{2,1,0:T(8,128)(2,1)S(1)} %copy-done), channel_id=1, source_target_pairs={{0,15},{1,14},{2,13},{3,12},{4,11},{5,10},{6,9},{7,8},{8,7},{9,6},... | collective-permute-start | bytes 4718600 | tf_op jit(solution)/shard_map/ppermute | solution.py:25
Sparse Core Ops, SparseCore 0:
  583.9 64.8 all-reduce.1
